TPU v7x, 128 devices: a whole 4x4x4 slice. The times are simulated.
128 devices in a mesh: dense: 32 (over x, z, core), attn: 4 (over y).
Axes of the slice: x: 4, y: 4, z: 4, core: 2. Of those that a mesh axis runs over, the one named last changes fastest.
Arguments:
- queries: bfloat16 [8192, 4096], P('dense', 'attn'), may hold values from -30 to 30
- keys: bfloat16 [8192, 1024], P('dense', 'attn'), may hold values from -13 to 13
- values: bfloat16 [8192, 1024], P('dense', 'attn'), may hold values from -24 to 24
- segments: int32 [8192], replicated, may hold values from 0 to 5, never falling along the last dimension, each value on 1 to 4096 neighbouring positions
- out_weight: bfloat16 [4096, 4096], P('attn', 'dense'), may hold values from -0.09375 to 0.09375
Outputs:
- projected: bfloat16 [8192, 4096], P('dense', 'attn')
All inputs are finite; a program needn't handle non-finite values.
Results may differ from a plain program's by a relative error of at most 0.012.
Values may be sent and summed in bfloat16 or wider, within the bound.
A program may use at most 128 MiB of HBM per device.

v0:
```python
import math
import jax
import jax.numpy as jnp
from jax import lax
from jax.sharding import PartitionSpec as P

HEAD_WIDTH = 128
NEGATIVE = -1e30


def attend(query_rows, positions, query_docs, keys, values, segments):
    token_count = query_rows.shape[0]
    kv_local = keys.shape[1] // HEAD_WIDTH
    head_group = query_rows.shape[1] // HEAD_WIDTH // kv_local
    blocks_count = max(token_count // 128, 1)
    block_rows = token_count // blocks_count
    inv_root = 1.0 / math.sqrt(HEAD_WIDTH)
    query_heads = query_rows.reshape(token_count, kv_local, head_group, HEAD_WIDTH)
    initial = tuple(
        (
            (
                jnp.full((kv_local, head_group, block_rows), NEGATIVE, jnp.float32),
                jnp.zeros((kv_local, head_group, block_rows), jnp.float32),
                jnp.zeros((kv_local, head_group, block_rows, HEAD_WIDTH), jnp.float32),
            )
            for which_block in range(blocks_count)
        )
    )
    key_piece = lax.all_gather(keys, "dense", axis=0, tiled=True)
    value_piece = lax.all_gather(values, "dense", axis=0, tiled=True)
    key_count = key_piece.shape[0]
    key_positions = jnp.arange(key_count, dtype=jnp.int32)
    key_heads = key_piece.reshape(key_count, kv_local, HEAD_WIDTH)
    value_heads = value_piece.reshape(key_count, kv_local, HEAD_WIDTH)
    updated = []
    for which_block in range(blocks_count):
        lower = which_block * block_rows
        upper = lower + block_rows
        visible = (query_docs[lower:upper, None] == segments[None, :]) & (
            key_positions[None, :] <= positions[lower:upper, None]
        )
        sliced = query_heads[lower:upper]

        def compute(state):
            row_max, totals, summed = state
            scores = (
                jnp.einsum("qgjd,kgd->gjqk", sliced, key_heads, preferred_element_type=jnp.float32)
                * inv_root
            )
            scores = jnp.where(visible, scores, NEGATIVE)
            new_max = jnp.maximum(row_max, jnp.max(scores, axis=-1))
            weights = jnp.where(visible, jnp.exp(scores - new_max[..., None]), 0.0)
            totals = jnp.sum(weights, axis=-1)
            summed = jnp.einsum(
                "gjqk,kgd->gjqd",
                weights.astype(jnp.bfloat16),
                value_heads,
                preferred_element_type=jnp.float32,
            )
            return (new_max, totals, summed)

        updated.append(
            lax.cond(jnp.any(visible), compute, lambda state: state, initial[which_block])
        )
    final = tuple(updated)
    outputs = []
    for state in final:
        outputs.append(state[2] / state[1][..., None])
    attended = jnp.concatenate(outputs, axis=2).astype(jnp.bfloat16)
    return attended.transpose(2, 0, 1, 3).reshape(token_count, kv_local * head_group * HEAD_WIDTH)


def project(attended, out_weight):
    partial_sums = jnp.dot(
        attended,
        lax.all_gather(out_weight, "dense", axis=1, tiled=True),
        preferred_element_type=jnp.float32,
    )
    return lax.psum_scatter(
        partial_sums.astype(jnp.bfloat16), "attn", scatter_dimension=1, tiled=True
    )


def shards(queries, keys, values, segments, out_weight):
    device_index = lax.axis_index("dense")
    token_count = queries.shape[0]
    positions = device_index * token_count + jnp.arange(token_count, dtype=jnp.int32)
    query_docs = lax.dynamic_slice_in_dim(segments, device_index * token_count, token_count)
    attended = attend(queries, positions, query_docs, keys, values, segments)
    projected = project(attended, out_weight)
    return projected


def solution(mesh):
    return jax.shard_map(
        shards,
        mesh=mesh,
        in_specs=(
            P("dense", "attn"),
            P("dense", "attn"),
            P("dense", "attn"),
            P(),
            P("attn", "dense"),
        ),
        out_specs=P("dense", "attn"),
        check_vma=False,
    )
```

profile of v0, /device:TPU:1, one launch (start us, length us, event | category | flops | bytes accessed | tf_op | source)
XLA Modules:
  0.0 251.5 jit_solution(4987157832332547177)
XLA Ops:
  6.5 0.0 all-gather.4.cloned.1.call-start
  6.5 1.7 copy.12
  8.2 0.0 all-gather.4.cloned.1.call-update
  8.2 0.0 all-gather.6.cloned.1.call-start
  8.3 1.6 copy.13
  9.9 0.0 all-gather.6.cloned.1.call-update
  9.9 0.0 all-gather.8.cloned.1.call-start
  10.0 0.7 all-gather.8.cloned.1.call-update
  10.7 0.0 reduce-scatter.2.cloned.1.call-start
  10.7 0.8 dynamic_slice.3
  11.5 4.9 %fusion.27 = (pred[]{:T(512)}, pred[]{:T(512)}, pred[128,8192]{0,1:T(8,128)(4,1)S(1)}, pred[128,8192]{0,1:T(8,128)(4,1)S(1)}) fusion(s32[128]{0:T(128)S(1)} %get-tuple-element.63, s32[8192]{0:T(1024)} %param.12, s32[128]{0:T(128)S(1)} %get-tuple-element.60, s32[128]{0:T(128)S(1)} %get-tuple-element.64, s32[128]{0:T(128)S(1)} %get-tuple-element.59), kind=kLoop, calls=%fused_computation.38 | loop fusion | flops 8388606 | bytes 2131970 | tf_op jit(solution)/shard_map/reduce_or | solution.py:63
  17.6 44.3 %all-gather.4.cloned.1.call-done = bf16[8192,256]{0,1:T(8,128)(2,1)} async-done(((bf16[256,256]{0,1:T(8,128)(2,1)}), bf16[8192,256]{0,1:T(8,128)(2,1)}) %all-gather.4.cloned.1.call-update) | async-done | bytes 4194320 | tf_op jit(solution)/shard_map/all_gather | solution.py:29
  61.9 50.4 %all-gather.6.cloned.1.call-done = bf16[8192,256]{0,1:T(8,128)(2,1)} async-done(((bf16[256,256]{0,1:T(8,128)(2,1)}), bf16[8192,256]{0,1:T(8,128)(2,1)}) %all-gather.6.cloned.1.call-update) | async-done | bytes 4194320 | tf_op jit(solution)/shard_map/all_gather | solution.py:30
  112.2 48.2 %conditional.2 = (f32[2,4,128]{2,1,0:T(4,128)S(1)}, f32[2,4,128,128]{2,3,1,0:T(8,128)S(1)}) conditional(s32[]{:T(128)} %convert_element_type.16, () %tuple.21, (pred[128,8192]{0,1:T(8,128)(4,1)S(1)}, bf16[256,1024]{1,0:T(8,128)(2,1)}, bf16[8192,2,128]{0,2,1:T(8,128)(2,1)}, bf16[8192,2,128]{0,2,1:T(8,128)(2,1)}) %tuple.54), branch_computations={%region_1.0_spmd, %region_2.5_spmd} | conditional | flops 4404018176 | bytes 114581520 | solution.py:63
  112.2 1.2 copy.14
  113.5 16.2 %fusion = (f32[2,4,128]{2,1,0:T(4,128)S(1)}, f32[2,8192,128,4]{2,1,3,0:T(8,128)}) fusion(pred[128,8192]{0,1:T(8,128)(4,1)S(1)} %get-tuple-element.25, bf16[128,2,4,128]{0,3,2,1:T(8,128)(2,1)S(1)} %bitcast.60, bf16[8192,2,128]{0,2,1:T(8,128)(2,1)} %get-tuple-element.43), kind=kOutput, calls=%fused_computation.2 | convolution fusion | flops 2172648448 | bytes 39063552 | tf_op jit(solution)/shard_map/cond/branch_1_fun/qgjd,kgd->gjqk/dot_general | solution.py:47
  129.8 15.5 %fusion.3 = f32[2,4,128,128]{2,3,1,0:T(8,128)S(1)} fusion(f32[2,8192,128,4]{2,1,3,0:T(8,128)} %get-tuple-element.54, f32[2,4,128]{2,1,0:T(4,128)S(1)} %broadcast_maximum_fusion, pred[128,8192]{0,1:T(8,128)(4,1)S(1)} %get-tuple-element.25, bf16[8192,2,128]{0,2,1:T(8,128)(2,1)} %get-tuple-element.44), kind=kOutput, calls=%fused_computation.5 | convolution fusion | flops 2189426688 | bytes 39325696 | tf_op jit(solution)/shard_map/cond | solution.py:63
  145.2 15.2 %fusion.2 = f32[2,4,128]{2,1,0:T(4,128)S(1)} fusion(f32[2,8192,128,4]{2,1,3,0:T(8,128)} %get-tuple-element.54, f32[2,4,128]{2,1,0:T(4,128)S(1)} %broadcast_maximum_fusion, pred[128,8192]{0,1:T(8,128)(4,1)S(1)} %get-tuple-element.25), kind=kLoop, calls=%fused_computation.4 | loop fusion | flops 41942016 | bytes 34611200 | tf_op jit(solution)/shard_map/cond/branch_1_fun/reduce_sum | solution.py:53
  160.4 47.9 %conditional.3 = (f32[2,4,128]{2,1,0:T(4,128)S(1)}, f32[2,4,128,128]{2,3,1,0:T(8,128)S(1)}) conditional(s32[]{:T(128)} %convert_element_type.17, () %tuple.23, (pred[128,8192]{0,1:T(8,128)(4,1)S(1)}, bf16[256,1024]{1,0:T(8,128)(2,1)}, bf16[8192,2,128]{0,2,1:T(8,128)(2,1)}, bf16[8192,2,128]{0,2,1:T(8,128)(2,1)}) %tuple.55), branch_computations={%region_6.7_spmd, %region_7.10_spmd} | conditional | flops 4404018176 | bytes 114581520 | solution.py:63
  160.6 1.2 copy.18
  161.9 16.3 %fusion.12 = (f32[2,4,128]{2,1,0:T(4,128)S(1)}, f32[2,8192,128,4]{2,1,3,0:T(8,128)}) fusion(pred[128,8192]{0,1:T(8,128)(4,1)S(1)} %get-tuple-element.29, bf16[128,2,4,128]{0,3,2,1:T(8,128)(2,1)S(1)} %bitcast.61, bf16[8192,2,128]{0,2,1:T(8,128)(2,1)} %get-tuple-element.47), kind=kOutput, calls=%fused_computation.16 | convolution fusion | flops 2172648448 | bytes 39063552 | tf_op jit(solution)/shard_map/cond/branch_1_fun/qgjd,kgd->gjqk/dot_general | solution.py:47
  178.3 15.4 %fusion.15 = f32[2,4,128,128]{2,3,1,0:T(8,128)S(1)} fusion(f32[2,8192,128,4]{2,1,3,0:T(8,128)} %get-tuple-element.56, f32[2,4,128]{2,1,0:T(4,128)S(1)} %broadcast_maximum_fusion.1, pred[128,8192]{0,1:T(8,128)(4,1)S(1)} %get-tuple-element.29, bf16[8192,2,128]{0,2,1:T(8,128)(2,1)} %get-tuple-element.48), kind=kOutput, calls=%fused_computation.19 | convolution fusion | flops 2189426688 | bytes 39325696 | tf_op jit(solution)/shard_map/cond | solution.py:63
  193.7 14.7 %fusion.14 = f32[2,4,128]{2,1,0:T(4,128)S(1)} fusion(f32[2,8192,128,4]{2,1,3,0:T(8,128)} %get-tuple-element.56, f32[2,4,128]{2,1,0:T(4,128)S(1)} %broadcast_maximum_fusion.1, pred[128,8192]{0,1:T(8,128)(4,1)S(1)} %get-tuple-element.29), kind=kLoop, calls=%fused_computation.18 | loop fusion | flops 41942016 | bytes 34611200 | tf_op jit(solution)/shard_map/cond/branch_1_fun/reduce_sum | solution.py:53
  208.3 0.1 divide_convert_fusion.1
  208.4 0.1 divide_convert_fusion
  208.5 0.1 pad_maximum_fusion
  208.5 0.0 all-gather.8.cloned.1.call-done
  208.6 7.1 %convolution_convert_fusion = bf16[256,4096]{1,0:T(8,128)(2,1)} fusion(bf16[256,1024]{0,1:T(8,128)(2,1)S(1)} %bitcast.59, bf16[1024,4096]{1,0:T(8,128)(2,1)} %all-gather.8.cloned.1.call-done), kind=kOutput, calls=%fused_computation.28 | convolution fusion | flops 2148532224 | bytes 11010048 | tf_op jit(solution)/shard_map/dot_general | solution.py:74
  215.7 0.0 reduce-scatter.2.cloned.1.call-update
  215.7 29.3 %reduce-scatter.2.cloned.1.call-done = bf16[256,1024]{1,0:T(8,128)(2,1)} async-done(((bf16[256,4096]{1,0:T(8,128)(2,1)}), bf16[256,1024]{1,0:T(8,128)(2,1)}) %reduce-scatter.2.cloned.1.call-update) | async-done | bytes 524304 | tf_op jit(solution)/shard_map/reduce_scatter | solution.py:79
  (6 shorter events, 0.1 us)
Async XLA Ops:
  6.5 55.3 %all-gather.4.cloned.1.call-start = ((), (), s32[]{:S(2)}) async-start(), calls=%async_computation.1 | async-start | bytes 4325376 | tf_op jit(solution)/shard_map/all_gather | solution.py:29
  8.2 104.0 %all-gather.6.cloned.1.call-start = ((), (), s32[]{:S(2)}) async-start(), calls=%async_computation.2 | async-start | bytes 4325376 | tf_op jit(solution)/shard_map/all_gather | solution.py:30
  9.9 198.6 %all-gather.8.cloned.1.call-start = ((), (), s32[]{:S(2)}) async-start(), calls=%async_computation.3 | async-start | bytes 8650752 | tf_op jit(solution)/shard_map/all_gather | solution.py:76
  10.7 234.3 %reduce-scatter.2.cloned.1.call-start = ((), (), s32[]{:S(2)}) async-start(), calls=%async_computation.4 | async-start | bytes 2621440 | tf_op jit(solution)/shard_map/reduce_scatter | solution.py:79
Sparse Core Ops, SparseCore 0:
  9.5 52.3 all-gather.3
  64.0 48.1 all-gather.5
  114.4 58.3 all-gather.7
  215.8 29.1 reduce-scatter.1
where the time goes:
time: 252 us
  waiting for transfers between devices  125 us (50%)
  matrix products  70.6 us (28%)
  other arithmetic  35 us (14%)
  between operations  14.3 us (6%)
  local copies, waits for them, and re-layouts  6.61 us (3%)
    all_gather x1, waiting for transfers between devices, attend(): value_piece = lax.all_gather(values, 'dense', axis=0, tiled=True)  50.4 us
    all_gather x1, waiting for transfers between devices, attend(): key_piece = lax.all_gather(keys, 'dense', axis=0, tiled=True)  44.3 us
    dot_general x2, matrix products, compute(): jnp.einsum('qgjd,kgd->gjqk', sliced, key_heads, preferred_element_type=jn...  32.6 us
    cond x2, matrix products, attend(): lax.cond(jnp.any(visible), compute, lambda state: state, initial[which_bl...  30.9 us
    reduce_sum x2, other arithmetic, compute(): totals = jnp.sum(weights, axis=-1)  29.9 us
    reduce_scatter x1, waiting for transfers between devices, project(): lax.psum_scatter(partial_sums.astype(jnp.bfloat16), 'attn', scatter_dimen...  29.3 us
    dot_general x1, matrix products, project(): jnp.dot(attended, lax.all_gather(out_weight, 'dense', axis=1, tiled=True)...  7.11 us
  transfers between devices with their start and end apart: 4, of which 3 were waited for; matrix products, arithmetic and copies ran while one was open for 41% of the time, Pallas kernels for 0%

commit v1 on v0

--- a/solution.py
+++ b/solution.py
@@ -26,8 +26,11 @@
             for which_block in range(blocks_count)
         )
     )
-    key_piece = lax.all_gather(keys, "dense", axis=0, tiled=True)
-    value_piece = lax.all_gather(values, "dense", axis=0, tiled=True)
+    key_piece, value_piece = jnp.split(
+        lax.all_gather(jnp.concatenate([keys, values], axis=1), "dense", axis=0, tiled=True),
+        [keys.shape[1]],
+        axis=1,
+    )
     key_count = key_piece.shape[0]
     key_positions = jnp.arange(key_count, dtype=jnp.int32)
     key_heads = key_piece.reshape(key_count, kv_local, HEAD_WIDTH)

time: 252 us -> 218 us (0.87)
  waiting for transfers between devices: 125 us -> 84.2 us
  local copies, waits for them, and re-layouts: 6.61 us -> 11.2 us
    all_gather x2 -> x1, waiting for transfers between devices: 94.6 us -> 55.1 us  [attend(): lax.all_gather(jnp.concatenate([keys, values], axis=1), 'dense', axis=0,...]
    split x0 -> x1, local copies, waits for them, and re-layouts: none -> 5.86 us  [attend(): jnp.split(lax.all_gather(jnp.concatenate([keys, values], axis=1), 'dense'...]
  transfers between devices with their start and end apart: 4 -> 3, of which waited for: 3 -> 2; matrix products, arithmetic and copies ran while one was open for 41% -> 50% of each run, Pallas kernels for 0% -> 0%
where the time goes in v1:
time: 218 us; the launch traced here: 217 us
  waiting for transfers between devices  84.2 us (39%)
  matrix products  70.7 us (32%)
  other arithmetic  36 us (17%)
  between operations  14.4 us (7%)
  local copies, waits for them, and re-layouts  11.2 us (5%)
    all_gather x1, waiting for transfers between devices, attend(): lax.all_gather(jnp.concatenate([keys, values], axis=1), 'dense', axis=0,...  55.1 us
    dot_general x2, matrix products, compute(): jnp.einsum('qgjd,kgd->gjqk', sliced, key_heads, preferred_element_type=jn...  32.2 us
    cond x2, matrix products, attend(): lax.cond(jnp.any(visible), compute, lambda state: state, initial[which_bl...  31.4 us
    reduce_sum x2, other arithmetic, compute(): totals = jnp.sum(weights, axis=-1)  30.1 us
    reduce_scatter x1, waiting for transfers between devices, project(): lax.psum_scatter(partial_sums.astype(jnp.bfloat16), 'attn', scatter_dimen...  28.4 us
    dot_general x1, matrix products, project(): jnp.dot(attended, lax.all_gather(out_weight, 'dense', axis=1, tiled=True)...  7.11 us
    split x1, local copies, waits for them, and re-layouts, attend(): jnp.split(lax.all_gather(jnp.concatenate([keys, values], axis=1), 'dense'...  5.86 us
    reduce_or x1, other arithmetic, attend(): jnp.any(visible)  4.95 us
  transfers between devices with their start and end apart: 3, of which 2 were waited for; matrix products, arithmetic and copies ran while one was open for 50% of the time, Pallas kernels for 0%

profile of v1, /device:TPU:1, one launch (start us, length us, event | category | flops | bytes accessed | tf_op | source)
XLA Modules:
  0.0 216.8 jit_solution(8706481943894244741)
XLA Ops:
  6.5 0.0 all-gather.3.cloned.1.call-start
  6.5 1.0 copy.12
  7.5 1.0 copy.13
  8.6 0.7 pad_maximum_fusion.1
  9.3 0.0 all-gather.3.cloned.1.call-update
  9.3 0.0 all-gather.5.cloned.1.call-start
  9.4 0.7 all-gather.5.cloned.1.call-update
  10.1 0.0 reduce-scatter.2.cloned.1.call-start
  10.1 0.8 dynamic_slice.3
  10.9 4.9 %fusion.27 = (pred[]{:T(512)}, pred[]{:T(512)}, pred[128,8192]{0,1:T(8,128)(4,1)S(1)}, pred[128,8192]{0,1:T(8,128)(4,1)S(1)}) fusion(s32[128]{0:T(128)S(1)} %get-tuple-element.65, s32[8192]{0:T(1024)} %param.12, s32[128]{0:T(128)S(1)} %get-tuple-element.62, s32[128]{0:T(128)S(1)} %get-tuple-element.66, s32[128]{0:T(128)S(1)} %get-tuple-element.61), kind=kLoop, calls=%fused_computation.39 | loop fusion | flops 8388606 | bytes 2131970 | tf_op jit(solution)/shard_map/reduce_or | solution.py:66
  17.1 55.1 %all-gather.3.cloned.1.call-done = bf16[8192,512]{0,1:T(8,128)(2,1)} async-done(((bf16[256,512]{0,1:T(8,128)(2,1)}), bf16[8192,512]{0,1:T(8,128)(2,1)}) %all-gather.3.cloned.1.call-update) | async-done | bytes 8388624 | tf_op jit(solution)/shard_map/all_gather | solution.py:30
  72.1 5.9 %fusion.28 = (bf16[8192,256]{0,1:T(8,128)(2,1)}, bf16[8192,256]{0,1:T(8,128)(2,1)}) fusion(bf16[8192,512]{0,1:T(8,128)(2,1)} %all-gather.3.cloned.1.call-done), kind=kLoop, calls=%fused_computation.40 | loop fusion | bytes 16777216 | tf_op jit(solution)/shard_map/split | solution.py:29
  78.0 48.8 %conditional.2 = (f32[2,4,128]{2,1,0:T(4,128)S(1)}, f32[2,4,128,128]{2,3,1,0:T(8,128)S(1)}) conditional(s32[]{:T(128)} %convert_element_type.16, () %tuple.21, (pred[128,8192]{0,1:T(8,128)(4,1)S(1)}, bf16[256,1024]{1,0:T(8,128)(2,1)}, bf16[8192,2,128]{0,2,1:T(8,128)(2,1)}, bf16[8192,2,128]{0,2,1:T(8,128)(2,1)}) %tuple.53), branch_computations={%region_1.0_spmd, %region_2.5_spmd} | conditional | flops 4404018176 | bytes 114581520 | solution.py:66
  78.0 1.2 copy.14
  79.3 16.1 %fusion = (f32[2,4,128]{2,1,0:T(4,128)S(1)}, f32[2,8192,128,4]{2,1,3,0:T(8,128)}) fusion(pred[128,8192]{0,1:T(8,128)(4,1)S(1)} %get-tuple-element.25, bf16[128,2,4,128]{0,3,2,1:T(8,128)(2,1)S(1)} %bitcast.62, bf16[8192,2,128]{0,2,1:T(8,128)(2,1)} %get-tuple-element.43), kind=kOutput, calls=%fused_computation.2 | convolution fusion | flops 2172648448 | bytes 39063552 | tf_op jit(solution)/shard_map/cond/branch_1_fun/qgjd,kgd->gjqk/dot_general | solution.py:50
  95.4 16.0 %fusion.3 = f32[2,4,128,128]{2,3,1,0:T(8,128)S(1)} fusion(f32[2,8192,128,4]{2,1,3,0:T(8,128)} %get-tuple-element.54, f32[2,4,128]{2,1,0:T(4,128)S(1)} %broadcast_maximum_fusion, pred[128,8192]{0,1:T(8,128)(4,1)S(1)} %get-tuple-element.25, bf16[8192,2,128]{0,2,1:T(8,128)(2,1)} %get-tuple-element.44), kind=kOutput, calls=%fused_computation.5 | convolution fusion | flops 2189426688 | bytes 39325696 | tf_op jit(solution)/shard_map/cond | solution.py:66
  111.4 15.4 %fusion.2 = f32[2,4,128]{2,1,0:T(4,128)S(1)} fusion(f32[2,8192,128,4]{2,1,3,0:T(8,128)} %get-tuple-element.54, f32[2,4,128]{2,1,0:T(4,128)S(1)} %broadcast_maximum_fusion, pred[128,8192]{0,1:T(8,128)(4,1)S(1)} %get-tuple-element.25), kind=kLoop, calls=%fused_computation.4 | loop fusion | flops 41942016 | bytes 34611200 | tf_op jit(solution)/shard_map/cond/branch_1_fun/reduce_sum | solution.py:56
  126.8 47.7 %conditional.3 = (f32[2,4,128]{2,1,0:T(4,128)S(1)}, f32[2,4,128,128]{2,3,1,0:T(8,128)S(1)}) conditional(s32[]{:T(128)} %convert_element_type.17, () %tuple.23, (pred[128,8192]{0,1:T(8,128)(4,1)S(1)}, bf16[256,1024]{1,0:T(8,128)(2,1)}, bf16[8192,2,128]{0,2,1:T(8,128)(2,1)}, bf16[8192,2,128]{0,2,1:T(8,128)(2,1)}) %tuple.54), branch_computations={%region_6.7_spmd, %region_7.10_spmd} | conditional | flops 4404018176 | bytes 114581520 | solution.py:66
  127.0 1.3 copy.18
  128.4 16.1 %fusion.12 = (f32[2,4,128]{2,1,0:T(4,128)S(1)}, f32[2,8192,128,4]{2,1,3,0:T(8,128)}) fusion(pred[128,8192]{0,1:T(8,128)(4,1)S(1)} %get-tuple-element.29, bf16[128,2,4,128]{0,3,2,1:T(8,128)(2,1)S(1)} %bitcast.63, bf16[8192,2,128]{0,2,1:T(8,128)(2,1)} %get-tuple-element.47), kind=kOutput, calls=%fused_computation.16 | convolution fusion | flops 2172648448 | bytes 39063552 | tf_op jit(solution)/shard_map/cond/branch_1_fun/qgjd,kgd->gjqk/dot_general | solution.py:50
  144.5 15.4 %fusion.15 = f32[2,4,128,128]{2,3,1,0:T(8,128)S(1)} fusion(f32[2,8192,128,4]{2,1,3,0:T(8,128)} %get-tuple-element.56, f32[2,4,128]{2,1,0:T(4,128)S(1)} %broadcast_maximum_fusion.1, pred[128,8192]{0,1:T(8,128)(4,1)S(1)} %get-tuple-element.29, bf16[8192,2,128]{0,2,1:T(8,128)(2,1)} %get-tuple-element.48), kind=kOutput, calls=%fused_computation.19 | convolution fusion | flops 2189426688 | bytes 39325696 | tf_op jit(solution)/shard_map/cond | solution.py:66
  159.9 14.7 %fusion.14 = f32[2,4,128]{2,1,0:T(4,128)S(1)} fusion(f32[2,8192,128,4]{2,1,3,0:T(8,128)} %get-tuple-element.56, f32[2,4,128]{2,1,0:T(4,128)S(1)} %broadcast_maximum_fusion.1, pred[128,8192]{0,1:T(8,128)(4,1)S(1)} %get-tuple-element.29), kind=kLoop, calls=%fused_computation.18 | loop fusion | flops 41942016 | bytes 34611200 | tf_op jit(solution)/shard_map/cond/branch_1_fun/reduce_sum | solution.py:56
  174.6 0.1 divide_convert_fusion.1
  174.6 0.1 divide_convert_fusion
  174.7 0.1 pad_maximum_fusion
  174.7 0.0 all-gather.5.cloned.1.call-done
  174.8 7.1 %convolution_convert_fusion = bf16[256,4096]{1,0:T(8,128)(2,1)} fusion(bf16[256,1024]{0,1:T(8,128)(2,1)S(1)} %bitcast.61, bf16[1024,4096]{1,0:T(8,128)(2,1)} %all-gather.5.cloned.1.call-done), kind=kOutput, calls=%fused_computation.28 | convolution fusion | flops 2148532224 | bytes 11010048 | tf_op jit(solution)/shard_map/dot_general | solution.py:77
  181.9 0.0 reduce-scatter.2.cloned.1.call-update
  181.9 28.4 %reduce-scatter.2.cloned.1.call-done = bf16[256,1024]{1,0:T(8,128)(2,1)} async-done(((bf16[256,4096]{1,0:T(8,128)(2,1)}), bf16[256,1024]{1,0:T(8,128)(2,1)}) %reduce-scatter.2.cloned.1.call-update) | async-done | bytes 524304 | tf_op jit(solution)/shard_map/reduce_scatter | solution.py:82
  (6 shorter events, 0.1 us)
Async XLA Ops:
  6.5 65.6 %all-gather.3.cloned.1.call-start = ((), (), s32[]{:S(2)}) async-start(), calls=%async_computation.1 | async-start | bytes 8650752 | tf_op jit(solution)/shard_map/all_gather | solution.py:30
  9.3 165.5 %all-gather.5.cloned.1.call-start = ((), (), s32[]{:S(2)}) async-start(), calls=%async_computation.2 | async-start | bytes 8650752 | tf_op jit(solution)/shard_map/all_gather | solution.py:79
  10.1 200.2 %reduce-scatter.2.cloned.1.call-start = ((), (), s32[]{:S(2)}) async-start(), calls=%async_computation.3 | async-start | bytes 2621440 | tf_op jit(solution)/shard_map/reduce_scatter | solution.py:82
Sparse Core Ops, SparseCore 0:
  9.5 62.5 all-gather.2
  74.3 58.5 all-gather.4
  182.0 28.2 reduce-scatter.1
